TPU v7x, 128 devices: a whole 4x4x4 slice. The times are simulated.
128 devices in a mesh: tile: 8 (over z, core), orbit: 16 (over y, x).
Axes of the slice: x: 4, y: 4, z: 4, core: 2. Of those that a mesh axis runs over, the one named last changes fastest.
Arguments:
- jacobians: bfloat16 [16384, 128, 3, 128], P(('tile', 'orbit')), may hold values from -1.5 to 1.5
- point_normals: float32 [16384, 6, 128], P(('tile', 'orbit')), as said below
- block_counts: int32 [128, 128], P(('tile', 'orbit')), may hold values from 1 to 128, 8192 in all within a row
- pair_owner: int32 [16384, 1], P(('tile', 'orbit')), may hold values from 0 to 15; in each aligned block of 128 rows (0 to 127, 128 to 255, ...) at most 16 rows name the same one
- pair_local: int32 [16384], P(('tile', 'orbit')), may hold values from 0 to 255
- crossing: int32 [16], replicated, may hold values from 0 to 15, as said below
Outputs:
- coupled: float32 [16, 256, 4096], P('orbit', 'tile')
Inputs may be any that keep to these rules, and one draw needn't show every extreme that they name: `point_normals`: each 3x3 block is symmetric, and in every row the diagonal entry exceeds the sum of the off-diagonal magnitudes by 0.2 or more. `pair_owner`: among the 128 rows of one device no owner appears more than 16 times. crossing[crossing[o]] = o and crossing[o] != o for every orbit o.
All inputs are finite; a program needn't handle non-finite values.
Results may differ from a plain program's by a relative error of at most 0.0029.
Values sent between devices are 32-bit elements; how exact they have to be, the bound alone decides.
No kernel may reach another device: no remote copies, remote signals or barrier semaphores. Data moves between devices by JAX's collectives and lax.ppermute only.
A program may use at most 128 MiB of HBM per device.

v0:
```python
import math

import jax
import jax.numpy as jnp
from jax import lax
from jax.sharding import PartitionSpec as P

PAIR_ORB = 256


def sent_together(arrays, axis, split_dim, concat_dim, along):
    widths = [math.prod(a.shape[along:]) for a in arrays]
    both = jnp.concatenate(
        [a.reshape(*a.shape[:along], w) for a, w in zip(arrays, widths)], axis=along
    )
    out = lax.all_to_all(both, axis, split_axis=split_dim, concat_axis=concat_dim, tiled=True)
    blocks = jnp.split(out, [sum(widths[:k]) for k in range(1, len(widths))], axis=along)
    return tuple((b.reshape(*out.shape[:along], *a.shape[along:]) for a, b in zip(arrays, blocks)))


def eliminate(jacobians, point_normals, counts, params):
    points = jacobians.shape[1]
    left_half = jacobians[..., :params]
    right_half = jacobians[..., params:].astype(jnp.float32)
    diag_one = point_normals[:, 0, :][:, :, None]
    diag_two = point_normals[:, 1, :][:, :, None]
    diag_three = point_normals[:, 2, :][:, :, None]
    off_ab = point_normals[:, 3, :][:, :, None]
    off_ac = point_normals[:, 4, :][:, :, None]
    off_bc = point_normals[:, 5, :][:, :, None]
    cof_aa = diag_two * diag_three - off_bc * off_bc
    cof_bb = diag_one * diag_three - off_ac * off_ac
    cof_cc = diag_one * diag_two - off_ab * off_ab
    cof_ab = off_ac * off_bc - off_ab * diag_three
    cof_ac = off_ab * off_bc - off_ac * diag_two
    cof_bc = off_ab * off_ac - diag_one * off_bc
    determinant = diag_one * cof_aa + off_ab * cof_ab + off_ac * cof_ac
    live_mask = (jnp.arange(points, dtype=jnp.int32)[None, :] < counts[:, None]).astype(jnp.float32)
    weight = live_mask[:, :, None] / determinant
    comp_a = right_half[:, :, 0, :]
    comp_b = right_half[:, :, 1, :]
    comp_c = right_half[:, :, 2, :]
    solved = jnp.stack(
        [
            (cof_aa * comp_a + cof_ab * comp_b + cof_ac * comp_c) * weight,
            (cof_ab * comp_a + cof_bb * comp_b + cof_bc * comp_c) * weight,
            (cof_ac * comp_a + cof_bc * comp_b + cof_cc * comp_c) * weight,
        ],
        axis=2,
    ).astype(jnp.bfloat16)
    blocks = jnp.einsum("spci,spcj->sij", left_half, solved, preferred_element_type=jnp.float32)
    return blocks.reshape(blocks.shape[0], params * params)


def local(jacobians, point_normals, block_counts, pair_owner, pair_local, crossing):
    slot_count = jacobians.shape[0]
    params = jacobians.shape[3] // 2
    square = params * params
    blocks = eliminate(jacobians, point_normals, block_counts[0], params)
    orbits = lax.axis_size("orbit")
    capacity = 2 * slot_count // orbits
    owners = pair_owner[:, 0]
    onehot = (owners[:, None] == jnp.arange(orbits, dtype=jnp.int32)[None, :]).astype(jnp.int32)
    before = jnp.cumsum(onehot, axis=0) - onehot
    slot_rank = jnp.sum(before * onehot, axis=1)
    target = owners * capacity + slot_rank
    outgoing = jnp.zeros((orbits * capacity, square), jnp.float32).at[target].set(blocks)
    outgoing = outgoing.reshape(orbits, capacity, square)
    labels = (
        jnp.full((orbits * capacity,), PAIR_ORB, jnp.float32)
        .at[target]
        .set(pair_local.astype(jnp.float32))
    )
    labels = labels.reshape(orbits, capacity)
    flipped = jnp.swapaxes(outgoing[crossing].reshape(orbits, capacity, params, params), 2, 3)
    flipped = flipped.reshape(orbits, capacity, square)
    arrived, arrived_flip, tag_rows, tag_flip = sent_together(
        (outgoing, flipped, labels, labels[crossing]), "orbit", 0, 0, 2
    )
    gathered = jnp.concatenate([arrived, arrived_flip], axis=0).reshape(-1, square)
    pair_tags = jnp.concatenate([tag_rows, tag_flip], axis=0).reshape(-1).astype(jnp.int32)
    dense_sums = jax.ops.segment_sum(gathered, pair_tags, num_segments=PAIR_ORB)
    owned_share = lax.psum_scatter(dense_sums, "tile", scatter_dimension=0, tiled=True)
    return owned_share[None]


def solution(mesh):
    in_specs = (
        P(("tile", "orbit"), None, None, None),
        P(("tile", "orbit"), None, None),
        P(("tile", "orbit"), None),
        P(("tile", "orbit"), None),
        P(("tile", "orbit")),
        P(),
    )
    out_specs = P("orbit", "tile", None)
    return jax.shard_map(local, mesh=mesh, in_specs=in_specs, out_specs=out_specs, check_vma=False)
```

profile of v0, /device:TPU:1, one launch (start us, length us, event | category | flops | bytes accessed | tf_op | source)
XLA Modules:
  0.0 275.8 jit_solution(14801570484373671213)
XLA Ops:
  6.5 0.7 fusion.25
  7.3 0.2 reduce_window_sum.11
  7.5 0.8 select_reduce_fusion
  8.3 0.7 fusion.26
  9.0 0.7 convert_element_type.33
  9.6 1.0 scatter_custom_fusion.1
  10.6 0.2 reshape_reshape.4
  10.8 0.1 reshape.270
  10.9 11.8 %slice.36 = bf16[128,128,3,64]{3,1,2,0:T(8,128)(2,1)} slice(bf16[128,128,3,128]{3,1,2,0:T(8,128)(2,1)} %param.6), slice={[0:128], [0:128], [0:3], [64:128]} | slice | bytes 12582912 | tf_op jit(solution)/shard_map/slice | solution.py:24
  22.7 12.2 %copy.33 = bf16[128,128,3,64]{1,3,2,0:T(8,128)(2,1)} copy(bf16[128,128,3,64]{3,1,2,0:T(8,128)(2,1)} %slice.36) | data formatting | bytes 12582912
  34.9 4.4 %convert_element_type.31 = f32[128,128,3,64]{1,3,2,0:T(8,128)S(1)} convert(bf16[128,128,3,64]{1,3,2,0:T(8,128)(2,1)} %copy.33) | non-fusion elementwise | flops 3145728 | bytes 18874368 | tf_op jit(solution)/shard_map/convert_element_type | solution.py:24
  39.3 0.1 fusion.19
  39.4 2.9 %multiply_convert_fusion.2 = (bf16[128,128,1,64]{1,3,2,0:T(8,128)(2,1)S(1)}, bf16[128,128,1,64]{1,3,2,0:T(8,128)(2,1)S(1)}, bf16[128,128,1,64]{1,3,2,0:T(8,128)(2,1)S(1)}) fusion(f32[128,128,3,64]{1,3,2,0:T(8,128)S(1)} %convert_element_type.31, f32[128,128]{1,0:T(8,128)S(1)} %get-tuple-element.19, f32[128,128]{1,0:T(8,128)S(1)} %get-tuple-element.20, ...), kind=kLoop, calls=%fused_computation.15 | loop fusion | flops 22020096 | bytes 19333120 | tf_op jit(solution)/shard_map/convert
  42.3 7.3 %fusion.7 = f32[128,64,64]{1,2,0:T(8,128)} fusion(bf16[128,128,3,128]{3,1,2,0:T(8,128)(2,1)} %param.6, bf16[128,128,1,64]{1,3,2,0:T(8,128)(2,1)S(1)} %get-tuple-element.13, bf16[128,128,1,64]{1,3,2,0:T(8,128)(2,1)S(1)} %get-tuple-element.12, bf16[128,128,1,64]{1,3,2,0:T(8,128)(2,1)S(1)} %get-tuple-element.11), kind=kOutput, calls=%fused_computation.16 | convolution fusion | flops 408944640 | bytes 20971520 | tf_op jit(solution)/shard_map/spci,spcj->sij/dot_general | solution.py:51
  49.6 4.5 %copy.27 = f32[128,64,64]{0,2,1:T(8,128)S(1)} copy(f32[128,64,64]{1,2,0:T(8,128)} %fusion.7) | data formatting | bytes 4194304 | tf_op jit(solution)/shard_map/spci,spcj->sij/dot_general | solution.py:51
  54.2 1.8 copy.28
  56.0 5.0 %scatter_custom_fusion = f32[256,4096]{1,0:T(8,128)} fusion(s32[128]{0:T(128)S(1)} %fusion.26, f32[128,4096]{1,0:T(8,128)} %copy.28, f32[]{:T(128)} %constant.5.clone.1), kind=kCustom, calls=%fused_computation.19 | custom fusion | bytes 4194816 | tf_op jit(solution)/shard_map/scatter | solution.py:67
  61.0 5.0 %gather_fusion = f32[16,16,4096]{2,1,0:T(8,128)} fusion(f32[16,16,4096]{2,1,0:T(8,128)} %bitcast.96, s32[1024]{0:T(1024)S(1)} %pad_clamp_fusion), kind=kCustom, calls=%fused_computation | custom fusion | bytes 8388672 | tf_op jit(solution)/shard_map/gather | solution.py:75
  65.9 7.8 %reshape.268 = f32[16,16,64,64]{3,2,1,0:T(8,128)} reshape(f32[16,16,4096]{2,1,0:T(8,128)} %gather_fusion) | data formatting | bytes 8388608 | tf_op jit(solution)/shard_map/reshape | solution.py:75
  73.8 9.2 %copy.29 = f32[16,16,64,64]{3,2,1,0:T(8,128)} copy(f32[16,16,64,64]{2,3,1,0:T(8,128)} %bitcast.98) | data formatting | bytes 8388608 | tf_op jit(solution)/shard_map/transpose | solution.py:75
  83.0 7.9 %reshape.269 = f32[16,16,4096]{2,1,0:T(8,128)} reshape(f32[16,16,64,64]{3,2,1,0:T(8,128)} %copy.29) | data formatting | bytes 8388608 | tf_op jit(solution)/shard_map/reshape | solution.py:76
  90.9 0.6 gather_fusion.1
  91.4 0.2 copy.31
  91.6 10.7 %concatenate.9 = f32[16,16,8194]{2,1,0:T(8,128)} concatenate(f32[16,16,4096]{2,1,0:T(8,128)} %bitcast.97, f32[16,16,4096]{2,1,0:T(8,128)} %reshape.269, f32[16,16,1]{2,1,0:T(8,128)S(1)} %reshape_reshape.4, f32[16,16,1]{2,1,0:T(8,128)S(1)} %copy.31), dimensions={2} | concatenate | bytes 16781312 | tf_op jit(solution)/shard_map/concatenate | solution.py:13
  102.3 103.7 %all_to_all.5 = f32[16,16,8194]{2,1,0:T(8,128)S(1)} all-to-all(f32[16,16,8194]{2,1,0:T(8,128)} %concatenate.9), channel_id=1, replica_groups=mesh['tile'=8,'orbit'=16] {'orbit'}, dimensions={0} | all-to-all | bytes 16781312 | tf_op jit(solution)/shard_map/all_to_all | solution.py:16
  206.0 3.3 %copy-done = f32[16,16,8194]{2,1,0:T(8,128)} copy-done((f32[16,16,8194]{2,1,0:T(8,128)}, f32[16,16,8194]{2,1,0:T(8,128)S(1)}, u32[]{:S(2)}) %copy-start) | copy-done | bytes 8390680
  209.3 0.2 slice_reduce_fusion.1
  209.5 0.1 reshape.309
  209.5 4.0 %fusion.33 = (f32[16,16,4096]{2,1,0:T(8,128)S(1)}, f32[16,16,4096]{2,1,0:T(8,128)S(1)}) fusion(f32[16,16,8194]{2,1,0:T(8,128)} %copy-done), kind=kLoop, calls=%fused_computation.60 | loop fusion | bytes 16777216 | tf_op jit(solution)/shard_map/split | solution.py:17
  213.6 3.8 %pad_maximum_fusion = f32[32,16,4096]{2,1,0:T(8,128)} fusion(f32[16,16,4096]{2,1,0:T(8,128)S(1)} %get-tuple-element.15, f32[16,16,4096]{2,1,0:T(8,128)S(1)} %get-tuple-element.14), kind=kLoop, calls=%fused_computation.7 | loop fusion | flops 2097152 | bytes 16777216 | tf_op jit(solution)/shard_map/concatenate | solution.py:80
  217.3 16.1 %scatter_custom_fusion.2 = f32[256,4096]{1,0:T(8,128)} fusion(s32[512]{0:T(512)S(1)} %reshape.309, f32[512,4096]{1,0:T(8,128)} %bitcast.100, f32[]{:T(128)} %constant.5.clone.1), kind=kCustom, calls=%fused_computation.17 | custom fusion | flops 2097152 | bytes 4194816 | tf_op jit(solution)/shard_map/scatter-add | solution.py:82
  233.5 35.4 %reduce-scatter.2.cloned.1.call-done = f32[32,4096]{1,0:T(8,128)} async-done(((f32[256,4096]{1,0:T(8,128)}), f32[32,4096]{1,0:T(8,128)}) %reduce-scatter.2.cloned.1.call-update) | async-done | bytes 524304 | tf_op jit(solution)/shard_map/reduce_scatter | solution.py:83
  (12 shorter events, 0.1 us)
Async XLA Ops:
  6.5 262.4 %reduce-scatter.2.cloned.1.call-start = ((), (), s32[]{:S(2)}) async-start(), calls=%async_computation.2 | async-start | bytes 4718592 | tf_op jit(solution)/shard_map/reduce_scatter | solution.py:83
  34.9 4.4 %copy-start.1 = (f32[128,6,128]{2,0,1:T(8,128)S(1)}, f32[128,6,128]{2,0,1:T(8,128)}, u32[]{:S(2)}) copy-start(f32[128,6,128]{2,0,1:T(8,128)} %param.7) | copy-start | bytes 1179652
  34.9 4.4 %copy-start.2 = (s32[1,128]{1,0:T(1,128)S(1)}, s32[1,128]{1,0:T(1,128)}, u32[]{:S(2)}) copy-start(s32[1,128]{1,0:T(1,128)} %param.8) | copy-start | bytes 1540
  49.6 6.4 %copy-start.3 = (s32[16]{0:T(128)S(1)}, s32[16]{0:T(128)}, u32[]{:S(2)}) copy-start(s32[16]{0:T(128)} %param.11) | copy-start | bytes 196
  206.0 3.3 %copy-start = (f32[16,16,8194]{2,1,0:T(8,128)}, f32[16,16,8194]{2,1,0:T(8,128)S(1)}, u32[]{:S(2)}) copy-start(f32[16,16,8194]{2,1,0:T(8,128)S(1)} %all_to_all.5) | copy-start | bytes 25171972
Sparse Core Ops, SparseCore 0:
  233.6 35.2 reduce-scatter.1
where the time goes:
time: 279 us; the launch traced here: 276 us
  blocking collectives  104 us (37%)
  local copies, waits for them, and re-layouts  85.5 us (31%)
  waiting for transfers between devices  35.4 us (13%)
  other arithmetic  30.3 us (11%)
  between operations  13.5 us (5%)
  matrix products  7.31 us (3%)
    all_to_all x1, blocking collectives, sent_together(): lax.all_to_all(both, axis, split_axis=split_dim, concat_axis=concat_dim,...  104 us
    reduce_scatter x1, waiting for transfers between devices, local(): lax.psum_scatter(dense_sums, 'tile', scatter_dimension=0, tiled=True)  35.4 us
    scatter-add x1, other arithmetic, local(): dense_sums = jax.ops.segment_sum(gathered, pair_tags, num_segments=PAIR_ORB)  16.1 us
    unnamed x9, local copies, waits for them, and re-layouts  15.5 us
    slice x1, local copies, waits for them, and re-layouts, eliminate(): right_half = jacobians[..., params:].astype(jnp.float32)  11.8 us
    concatenate x1, local copies, waits for them, and re-layouts, sent_together(): jnp.concatenate([a.reshape(*a.shape[:along], w) for a, w in zip(arrays, w...  10.7 us
    transpose x1, local copies, waits for them, and re-layouts, local(): jnp.swapaxes(outgoing[crossing].reshape(orbits, capacity, params, params)...  9.23 us
    reshape x1, local copies, waits for them, and re-layouts, local(): flipped = flipped.reshape(orbits, capacity, square)  7.89 us
  transfers between devices with their start and end apart: 1, of which 1 were waited for; matrix products, arithmetic and copies ran while one was open for 0% of the time, Pallas kernels for 0%

commit v1 on v0

v1 whole, which is shorter than its diff:
```python
import functools

import jax
import jax.numpy as jnp
from jax import lax
from jax.experimental import pallas as pl
from jax.experimental.pallas import tpu as pltpu
from jax.sharding import PartitionSpec as P

DEVICES = 128
SLOTS = 128
PTS = 128
PARAMS = 64
ORBITS = 16
PAIR_ORB = 256
TILES = 8
ELEMS = PARAMS * PARAMS // DEVICES
ROWS = ELEMS + 1
STEP_SLOTS = 8
STEP_SRC = 16
NT = (((1,), (1,)), ((), ()))


def dot_nt(a, b):
    return lax.dot_general(a, b, NT, preferred_element_type=jnp.float32)


def eye(n):
    r = lax.broadcasted_iota(jnp.int32, (n, n), 0)
    c = lax.broadcasted_iota(jnp.int32, (n, n), 1)
    return jnp.where(r == c, 1.0, 0.0).astype(jnp.bfloat16)


def crossing_ranks(cross, ranks):
    seen = jnp.int32(0)
    for o in range(ORBITS):
        ranks[o] = seen
        seen = seen + (cross[o] > o).astype(jnp.int32)


def pair_of(o, cross, ranks):
    return ranks[jnp.minimum(o, cross[o])]


def blocks_kernel(counts, owner, cross, jac, normals, owner_row, local_row, out, held, ranks):
    step = pl.program_id(0)
    w11, w22, w33 = normals[0], normals[1], normals[2]
    w12, w13, w23 = normals[3], normals[4], normals[5]
    c11 = w22 * w33 - w23 * w23
    c22 = w11 * w33 - w13 * w13
    c33 = w11 * w22 - w12 * w12
    c12 = w13 * w23 - w12 * w33
    c13 = w12 * w23 - w13 * w22
    c23 = w12 * w13 - w11 * w23
    det = w11 * c11 + w12 * c12 + w13 * c13
    sub = lax.broadcasted_iota(jnp.int32, (STEP_SLOTS, PTS), 0)
    place = lax.broadcasted_iota(jnp.int32, (STEP_SLOTS, PTS), 1)
    limit = jnp.zeros((STEP_SLOTS, PTS), jnp.int32)
    for i in range(STEP_SLOTS):
        limit = jnp.where(sub == i, counts[step * STEP_SLOTS + i], limit)
    weight = jnp.where(place < limit, 1.0, 0.0) / det
    c11, c22, c33 = c11 * weight, c22 * weight, c33 * weight
    c12, c13, c23 = c12 * weight, c13 * weight, c23 * weight
    ident = eye(2 * PARAMS)
    for i in range(STEP_SLOTS):
        slot = step * STEP_SLOTS + i
        turned = dot_nt(ident, jac[i])
        left = turned[:PARAMS].astype(jnp.bfloat16)
        right = turned[PARAMS:]
        one, two, three = right[:, :PTS], right[:, PTS : 2 * PTS], right[:, 2 * PTS :]
        row = slice(i, i + 1)
        solved = jnp.concatenate(
            [
                c11[row] * one + c12[row] * two + c13[row] * three,
                c12[row] * one + c22[row] * two + c23[row] * three,
                c13[row] * one + c23[row] * two + c33[row] * three,
            ],
            axis=1,
        ).astype(jnp.bfloat16)
        mine = owner[slot]
        upper = mine > cross[mine]
        a = jnp.where(upper, left, solved)
        b = jnp.where(upper, solved, left)
        held[pl.ds(slot, PARAMS, stride=SLOTS), :] = dot_nt(a, b)

    @pl.when(step == pl.num_programs(0) - 1)
    def _():
        small = eye(PARAMS)
        half = PARAMS // 2
        for col in range(PARAMS):
            lines = held[col * SLOTS : (col + 1) * SLOTS, :].astype(jnp.bfloat16)
            start = (col // half) * PARAMS * ROWS + col % half
            out[pl.ds(start, PARAMS, stride=ROWS), :] = dot_nt(small, lines)
        crossing_ranks(cross, ranks)
        names = owner_row[...]
        ids = jnp.zeros_like(names)
        for o in range(ORBITS):
            ids = jnp.where(names == o, pair_of(o, cross, ranks) * PAIR_ORB, ids)
        ids = (ids + local_row[...]).astype(jnp.float32)
        out[pl.ds(ELEMS, DEVICES, stride=ROWS), :] = jnp.broadcast_to(ids, (DEVICES, SLOTS))


def sum_kernel(cross, arrived, out, hot, values, total, ranks):
    step = pl.program_id(0)

    @pl.when(step == 0)
    def _():
        total[...] = jnp.zeros_like(total)

    lines = lax.broadcasted_iota(jnp.int32, (PAIR_ORB, SLOTS), 0)
    for i in range(STEP_SRC):
        base = i * ROWS
        piece = arrived[base : base + ELEMS, :]
        ids = arrived[base + ELEMS : base + ROWS, :].astype(jnp.int32)
        local = ids & (PAIR_ORB - 1)
        line = (ids >> 8) * 32 + (local >> 6) * 8 + (local & 7)
        group = (local >> 3) & 7
        at = slice(i * SLOTS, (i + 1) * SLOTS)
        hot[:, at] = jnp.where(lines == line, 1.0, 0.0).astype(jnp.bfloat16)
        for g in range(8):
            values[g * ELEMS : (g + 1) * ELEMS, at] = jnp.where(group == g, piece, 0.0).astype(jnp.bfloat16)
    total[...] += dot_nt(hot[...], values[...])

    @pl.when(step == pl.num_programs(0) - 1)
    def _():
        crossing_ranks(cross, ranks)
        for o in range(ORBITS):
            pair = pair_of(o, cross, ranks)
            for t in range(TILES):
                start = pl.multiple_of(pair * 32 + (t >> 1) * 8, 8)
                dest = (t * ORBITS + o) * 8
                out[dest : dest + 8, :] = total[pl.ds(start, 8), (t & 1) * 128 : (t & 1) * 128 + 128]


def place_kernel(cross, arrived, out, turned):
    me = lax.axis_index("orbit")
    upper = me > cross[me]
    lane = lax.broadcasted_iota(jnp.int32, (8, 128), 1)

    @pl.when(jnp.logical_not(upper))
    def _():
        band = lane // 32
        for tile in range(32):
            v = []
            for g in range(4):
                d = (g % 2) * PARAMS + 2 * tile + g // 2
                v.append(arrived[d * 8 : d * 8 + 8, :])
            moved = []
            for r in range(4):
                z = v[r]
                for h in range(1, 4):
                    z = jnp.where(band == h, v[(h + r) % 4], z)
                moved.append(z if r == 0 else pltpu.roll(z, 32 * r, 1))
            for h in range(4):
                u = moved[(0 - h) % 4]
                for g in range(1, 4):
                    u = jnp.where(band == g, moved[(g - h) % 4], u)
                start = (h * 32 + tile) * 8
                out[start : start + 8, :] = u

    @pl.when(upper)
    def _():
        low = lax.broadcasted_iota(jnp.int32, (64, 128), 1) < PARAMS
        for j in range(8):
            turned[...] = arrived[pl.ds(j, 128, stride=8), :].T
            even = turned[pl.ds(0, 64, stride=2), :]
            odd = turned[pl.ds(1, 64, stride=2), :]
            halves = (
                jnp.where(low, even, pltpu.roll(odd, PARAMS, 1)),
                jnp.where(low, pltpu.roll(even, PARAMS, 1), odd),
            )
            for h in range(4):
                for half in range(2):
                    start = h * 256 + half * 128 + j
                    out[pl.ds(start, 16, stride=8), :] = halves[half][h * 16 : h * 16 + 16]


def smem():
    return pl.BlockSpec(memory_space=pltpu.SMEM)


def exchange(x):
    return lax.all_to_all(x, ("tile", "orbit"), split_axis=0, concat_axis=0, tiled=True)


def make_blocks(jacobians, point_normals, counts, owners, locals_, crossing):
    jac = jnp.transpose(jacobians, (0, 2, 1, 3)).reshape(SLOTS, 3 * PTS, 2 * PARAMS)
    normals = jnp.transpose(point_normals, (1, 0, 2))
    row = pl.BlockSpec((1, SLOTS), lambda i: (0, 0))
    return pl.pallas_call(
        blocks_kernel,
        grid=(SLOTS // STEP_SLOTS,),
        in_specs=[
            smem(),
            smem(),
            smem(),
            pl.BlockSpec((STEP_SLOTS, 3 * PTS, 2 * PARAMS), lambda i: (i, 0, 0)),
            pl.BlockSpec((6, STEP_SLOTS, PTS), lambda i: (0, i, 0)),
            row,
            row,
        ],
        out_specs=pl.BlockSpec((DEVICES * ROWS, SLOTS), lambda i: (0, 0)),
        out_shape=jax.ShapeDtypeStruct((DEVICES * ROWS, SLOTS), jnp.float32),
        scratch_shapes=[
            pltpu.VMEM((PARAMS * SLOTS, PARAMS), jnp.float32),
            pltpu.SMEM((ORBITS,), jnp.int32),
        ],
        name="blocks",
    )(counts, owners, crossing, jac, normals, owners.reshape(1, SLOTS), locals_.reshape(1, SLOTS))


def sum_pairs(arrived, crossing):
    return pl.pallas_call(
        sum_kernel,
        grid=(DEVICES // STEP_SRC,),
        in_specs=[smem(), pl.BlockSpec((STEP_SRC * ROWS, SLOTS), lambda i: (i, 0))],
        out_specs=pl.BlockSpec((DEVICES * 8, 128), lambda i: (0, 0)),
        out_shape=jax.ShapeDtypeStruct((DEVICES * 8, 128), jnp.float32),
        scratch_shapes=[
            pltpu.VMEM((PAIR_ORB, STEP_SRC * SLOTS), jnp.bfloat16),
            pltpu.VMEM((PAIR_ORB, STEP_SRC * SLOTS), jnp.bfloat16),
            pltpu.VMEM((PAIR_ORB, PAIR_ORB), jnp.float32),
            pltpu.SMEM((ORBITS,), jnp.int32),
        ],
        name="sum_pairs",
    )(crossing, arrived)


def place(arrived, crossing):
    return pl.pallas_call(
        place_kernel,
        in_specs=[smem(), pl.BlockSpec(memory_space=pltpu.VMEM)],
        out_specs=pl.BlockSpec(memory_space=pltpu.VMEM),
        out_shape=jax.ShapeDtypeStruct((DEVICES * 8, 128), jnp.float32),
        scratch_shapes=[pltpu.VMEM((128, 128), jnp.float32)],
        name="place",
    )(crossing, arrived)


def local(jacobians, point_normals, block_counts, pair_owner, pair_local, crossing):
    sent = make_blocks(
        jacobians, point_normals, block_counts.reshape(SLOTS), pair_owner.reshape(SLOTS), pair_local, crossing
    )
    arrived = exchange(sent.reshape(DEVICES, ROWS, 1, SLOTS))
    sums = sum_pairs(arrived.reshape(DEVICES * ROWS, SLOTS), crossing)
    mine = exchange(sums.reshape(DEVICES, 8, 128))
    out = place(mine.reshape(DEVICES * 8, 128), crossing)
    out = jnp.transpose(out.reshape(4, 32, 8, 128), (0, 2, 1, 3))
    return out.reshape(1, PAIR_ORB // TILES, PARAMS * PARAMS)


def solution(mesh):
    both = ("tile", "orbit")
    in_specs = (
        P(both, None, None, None),
        P(both, None, None),
        P(both, None),
        P(both, None),
        P(both),
        P(),
    )
    return jax.shard_map(local, mesh=mesh, in_specs=in_specs, out_specs=P("orbit", "tile", None), check_vma=False)
```

time: 279 us -> 107 us (0.38)
  local copies, waits for them, and re-layouts: 85.5 us -> 0 us
  Pallas kernels: 0 us -> 44.7 us
  blocking collectives: 104 us -> 61.5 us
  waiting for transfers between devices: 35.4 us -> 0 us
  other arithmetic: 30.3 us -> 0 us
  between operations: 13.5 us -> 0.01 us
  matrix products: 7.31 us -> 0 us
    pallas_call x0 -> x3, Pallas kernels: none -> 44.7 us  [the longest x1 33.4 us: make_blocks(): pl.pallas_call(blocks_kernel, grid=(SLOTS // STEP_SLOTS,), in_specs=[smem...]
    all_to_all x1 -> x2, blocking collectives: 104 us -> 61.5 us  [exchange(): lax.all_to_all(x, ('tile', 'orbit'), split_axis=0, concat_axis=0, tiled=T...]
    reduce_scatter x1 -> x0, waiting for transfers between devices: 35.4 us -> none  [local(): lax.psum_scatter(dense_sums, 'tile', scatter_dimension=0, tiled=True)]
    reshape x5 -> x0, local copies, waits for them, and re-layouts: 17.8 us -> none  [the longest x1 7.89 us: local(): flipped = flipped.reshape(orbits, capacity, square)]
    scatter-add x1 -> x0, other arithmetic: 16.1 us -> none  [local(): dense_sums = jax.ops.segment_sum(gathered, pair_tags, num_segments=PAIR_ORB)]
    unnamed x9 -> x0, local copies, waits for them, and re-layouts: 15.5 us -> none
    slice x1 -> x0, local copies, waits for them, and re-layouts: 11.8 us -> none  [eliminate(): right_half = jacobians[..., params:].astype(jnp.float32)]
    concatenate x1 -> x0, local copies, waits for them, and re-layouts: 10.7 us -> none  [sent_together(): jnp.concatenate([a.reshape(*a.shape[:along], w) for a, w in zip(arrays, w...]
  transfers between devices with their start and end apart: 1 -> 0, of which waited for: 1 -> 0; matrix products, arithmetic and copies ran while one was open for 0% -> 0% of each run, Pallas kernels for 0% -> 0%
where the time goes in v1:
time: 107 us; the launch traced here: 106 us
  blocking collectives  61.5 us (57%)
  Pallas kernels  44.7 us (42%)
    all_to_all x2, blocking collectives, exchange(): lax.all_to_all(x, ('tile', 'orbit'), split_axis=0, concat_axis=0, tiled=T...  61.5 us
    pallas_call x1, Pallas kernels, make_blocks(): pl.pallas_call(blocks_kernel, grid=(SLOTS // STEP_SLOTS,), in_specs=[smem...  33.4 us
    pallas_call x1, Pallas kernels, sum_pairs(): pl.pallas_call(sum_kernel, grid=(DEVICES // STEP_SRC,), in_specs=[smem(),...  9.25 us

profile of v1, /device:TPU:1, one launch (start us, length us, event | category | flops | bytes accessed | tf_op | source)
XLA Modules:
  0.0 106.1 jit_solution(10536600808596748502)
XLA Ops:
  0.0 33.4 %blocks.1 = f32[4224,128]{1,0:T(8,128)} custom-call(s32[128]{0:T(128)} %bitcast.25, s32[128]{0:T(128)} %bitcast.23, s32[16]{0:T(128)} %cross.5, bf16[128,384,128]{2,1,0:T(8,128)(2,1)} %bitcast.17, f32[6,128,128]{2,1,0:T(8,128)} %bitcast.22, s32[1,128]{1,0:T(1,128)} %bitcast.24, s32[1,128]{1,0:T(1,128)} %bitcast.26), custom_call_target="tpu_custom_call" | custom-call | tf_op jit(solution)/shard_map/blocks/pallas_call | solution.py:190
  33.4 42.0 %all_to_all.10 = f32[128,33,1,128]{3,2,1,0:T(1,128)} all-to-all(f32[128,33,1,128]{3,2,1,0:T(1,128)} %bitcast.18), channel_id=1, replica_groups=mesh['tile'=8,'orbit'=16] {'tile','orbit'}, dimensions={0} | all-to-all | bytes 4325376 | tf_op jit(solution)/shard_map/all_to_all | solution.py:183
  75.4 9.2 %sum_pairs.1 = f32[1024,128]{1,0:T(8,128)} custom-call(s32[16]{0:T(128)} %cross.5, f32[4224,128]{1,0:T(8,128)} %bitcast.19), custom_call_target="tpu_custom_call" | custom-call | tf_op jit(solution)/shard_map/sum_pairs/pallas_call | solution.py:213
  84.6 19.5 %all_to_all.11 = f32[128,8,128]{2,1,0:T(8,128)} all-to-all(f32[128,8,128]{2,1,0:T(8,128)} %bitcast.21), channel_id=1, replica_groups=mesh['tile'=8,'orbit'=16] {'tile','orbit'}, dimensions={0} | all-to-all | bytes 1048576 | tf_op jit(solution)/shard_map/all_to_all | solution.py:183
  104.1 2.0 %place.1 = f32[1024,128]{1,0:T(8,128)} custom-call(s32[16]{0:T(128)} %cross.5, f32[1024,128]{1,0:T(8,128)} %bitcast.20), custom_call_target="tpu_custom_call" | custom-call | tf_op jit(solution)/shard_map/place/pallas_call | solution.py:230

commit v2 on v1

v2 whole, which is shorter than its diff:
```python
import jax
import jax.numpy as jnp
from jax import lax
from jax.experimental import pallas as pl
from jax.experimental.pallas import tpu as pltpu
from jax.sharding import PartitionSpec as P

DEVICES = 128
SLOTS = 128
PTS = 128
PARAMS = 64
ORBITS = 16
PAIR_ORB = 256
TILES = 8
ELEMS = PARAMS * PARAMS // DEVICES
ROWS = ELEMS + 1
STEP_SLOTS = 8
STEP_SRC = 16
NT = (((1,), (1,)), ((), ()))


def dot_nt(a, b):
    return lax.dot_general(a, b, NT, preferred_element_type=jnp.float32)


def eye(n):
    r = lax.broadcasted_iota(jnp.int32, (n, n), 0)
    c = lax.broadcasted_iota(jnp.int32, (n, n), 1)
    return jnp.where(r == c, 1.0, 0.0).astype(jnp.bfloat16)


def crossing_ranks(cross, ranks):
    seen = jnp.int32(0)
    for o in range(ORBITS):
        ranks[o] = seen
        seen = seen + (cross[o] > o).astype(jnp.int32)


def pair_of(o, cross, ranks):
    return ranks[jnp.minimum(o, cross[o])]


def blocks_kernel(counts, owner, cross, jac_hbm, normals_hbm, owner_row, local_row, out, jac, normals, held, ranks, sems):
    steps = SLOTS // STEP_SLOTS
    copy_normals = pltpu.make_async_copy(normals_hbm, normals, sems.at[steps])
    copy_normals.start()

    def part(step):
        at = pl.ds(step * STEP_SLOTS, STEP_SLOTS)
        return pltpu.make_async_copy(jac_hbm.at[at], jac.at[at], sems.at[step])

    for step in range(steps):
        part(step).start()
    crossing_ranks(cross, ranks)
    names = owner_row[...]
    ids = jnp.zeros_like(names)
    for o in range(ORBITS):
        ids = jnp.where(names == o, pair_of(o, cross, ranks) * PAIR_ORB, ids)
    ids = (ids + local_row[...]).astype(jnp.float32)
    out[pl.ds(ELEMS, DEVICES, stride=ROWS), :] = jnp.broadcast_to(ids, (DEVICES, SLOTS))
    copy_normals.wait()
    sub = lax.broadcasted_iota(jnp.int32, (STEP_SLOTS, PTS), 0)
    place = lax.broadcasted_iota(jnp.int32, (STEP_SLOTS, PTS), 1)

    def body(step, carry):
        base = pl.multiple_of(step * STEP_SLOTS, STEP_SLOTS)
        w11, w22, w33, w12, w13, w23 = (normals[q, pl.ds(base, STEP_SLOTS), :] for q in range(6))
        c11 = w22 * w33 - w23 * w23
        c22 = w11 * w33 - w13 * w13
        c33 = w11 * w22 - w12 * w12
        c12 = w13 * w23 - w12 * w33
        c13 = w12 * w23 - w13 * w22
        c23 = w12 * w13 - w11 * w23
        det = w11 * c11 + w12 * c12 + w13 * c13
        limit = jnp.zeros((STEP_SLOTS, PTS), jnp.int32)
        for i in range(STEP_SLOTS):
            limit = jnp.where(sub == i, counts[base + i], limit)
        weight = jnp.where(place < limit, 1.0, 0.0) / det
        c11, c22, c33 = c11 * weight, c22 * weight, c33 * weight
        c12, c13, c23 = c12 * weight, c13 * weight, c23 * weight
        part(step).wait()
        for i in range(STEP_SLOTS):
            slot = base + i
            turned = jac[slot].T
            left = turned[:PARAMS]
            right = turned[PARAMS:].astype(jnp.float32)
            one, two, three = right[:, :PTS], right[:, PTS : 2 * PTS], right[:, 2 * PTS :]
            row = slice(i, i + 1)
            solved = jnp.concatenate(
                [
                    c11[row] * one + c12[row] * two + c13[row] * three,
                    c12[row] * one + c22[row] * two + c23[row] * three,
                    c13[row] * one + c23[row] * two + c33[row] * three,
                ],
                axis=1,
            ).astype(jnp.bfloat16)
            mine = owner[slot]
            upper = mine > cross[mine]
            a = jnp.where(upper, left, solved)
            b = jnp.where(upper, solved, left)
            held[pl.ds(slot, PARAMS, stride=SLOTS + 1), :] = dot_nt(a, b)
        return carry

    lax.fori_loop(0, steps, body, 0)
    half = PARAMS // 2
    for col in range(PARAMS):
        lines = held[col * (SLOTS + 1) : col * (SLOTS + 1) + SLOTS, :]
        start = (col // half) * PARAMS * ROWS + col % half
        out[pl.ds(start, PARAMS, stride=ROWS), :] = lines.T


def sum_kernel(cross, arrived, out, hot, values, total, ranks):
    lines = lax.broadcasted_iota(jnp.int32, (PAIR_ORB, SLOTS), 0)
    total[...] = jnp.zeros_like(total)

    def body(step, carry):
        for i in range(STEP_SRC):
            base = (step * STEP_SRC + i) * ROWS
            piece = arrived[pl.ds(base, ELEMS), :]
            ids = arrived[pl.ds(base + ELEMS, 1), :].astype(jnp.int32)
            local = ids & (PAIR_ORB - 1)
            line = (ids >> 8) * 32 + (local >> 6) * 8 + (local & 7)
            group = (local >> 3) & 7
            at = slice(i * SLOTS, (i + 1) * SLOTS)
            hot[:, at] = jnp.where(lines == line, 1.0, 0.0).astype(jnp.bfloat16)
            for g in range(8):
                values[g * ELEMS : (g + 1) * ELEMS, at] = jnp.where(group == g, piece, 0.0).astype(jnp.bfloat16)
        total[...] += dot_nt(hot[...], values[...])
        return carry

    lax.fori_loop(0, DEVICES // STEP_SRC, body, 0)
    crossing_ranks(cross, ranks)
    for o in range(ORBITS):
        pair = pair_of(o, cross, ranks)
        for t in range(TILES):
            start = pl.multiple_of(pair * 32 + (t >> 1) * 8, 8)
            dest = (t * ORBITS + o) * 8
            out[dest : dest + 8, :] = total[pl.ds(start, 8), (t & 1) * 128 : (t & 1) * 128 + 128]


def place_kernel(cross, arrived, out, turned):
    me = lax.axis_index("orbit")
    upper = me > cross[me]
    lane = lax.broadcasted_iota(jnp.int32, (8, 128), 1)

    @pl.when(jnp.logical_not(upper))
    def _():
        band = lane // 32
        for tile in range(32):
            v = []
            for g in range(4):
                d = (g % 2) * PARAMS + 2 * tile + g // 2
                v.append(arrived[d * 8 : d * 8 + 8, :])
            moved = []
            for r in range(4):
                z = v[r]
                for h in range(1, 4):
                    z = jnp.where(band == h, v[(h + r) % 4], z)
                moved.append(z if r == 0 else pltpu.roll(z, 32 * r, 1))
            for h in range(4):
                u = moved[(0 - h) % 4]
                for g in range(1, 4):
                    u = jnp.where(band == g, moved[(g - h) % 4], u)
                start = (h * 32 + tile) * 8
                out[start : start + 8, :] = u

    @pl.when(upper)
    def _():
        low = lax.broadcasted_iota(jnp.int32, (64, 128), 1) < PARAMS
        for j in range(8):
            turned[...] = arrived[pl.ds(j, 128, stride=8), :].T
            even = turned[pl.ds(0, 64, stride=2), :]
            odd = turned[pl.ds(1, 64, stride=2), :]
            halves = (
                jnp.where(low, even, pltpu.roll(odd, PARAMS, 1)),
                jnp.where(low, pltpu.roll(even, PARAMS, 1), odd),
            )
            for h in range(4):
                for half in range(2):
                    start = h * 256 + half * 128 + j
                    out[pl.ds(start, 16, stride=8), :] = halves[half][h * 16 : h * 16 + 16]


def smem():
    return pl.BlockSpec(memory_space=pltpu.SMEM)


def exchange(x):
    return lax.all_to_all(x, ("tile", "orbit"), split_axis=0, concat_axis=0, tiled=True)


def in_vmem():
    return pl.BlockSpec(memory_space=pltpu.VMEM)


def in_hbm():
    return pl.BlockSpec(memory_space=pl.ANY)


def hbm(x):
    return pltpu.with_memory_space_constraint(x, pltpu.HBM)


def make_blocks(jacobians, point_normals, counts, owners, locals_, crossing):
    jac = jnp.transpose(jacobians, (0, 2, 1, 3)).reshape(SLOTS, 3 * PTS, 2 * PARAMS)
    normals = jnp.transpose(point_normals, (1, 0, 2))
    return pl.pallas_call(
        blocks_kernel,
        in_specs=[smem(), smem(), smem(), in_hbm(), in_hbm(), in_vmem(), in_vmem()],
        out_specs=in_vmem(),
        out_shape=pltpu.VMEM((DEVICES * ROWS, SLOTS), jnp.float32),
        scratch_shapes=[
            pltpu.VMEM((SLOTS, 3 * PTS, 2 * PARAMS), jnp.bfloat16),
            pltpu.VMEM((6, SLOTS, PTS), jnp.float32),
            pltpu.VMEM((PARAMS * (SLOTS + 1), PARAMS), jnp.float32),
            pltpu.SMEM((ORBITS,), jnp.int32),
            pltpu.SemaphoreType.DMA((SLOTS // STEP_SLOTS + 1,)),
        ],
        compiler_params=pltpu.CompilerParams(vmem_limit_bytes=24 << 20),
        name="blocks",
    )(*map(hbm, (counts, owners, crossing, jac, normals, owners.reshape(1, SLOTS), locals_.reshape(1, SLOTS))))


def sum_pairs(arrived, crossing):
    return pl.pallas_call(
        sum_kernel,
        in_specs=[smem(), in_vmem()],
        out_specs=in_vmem(),
        out_shape=pltpu.VMEM((DEVICES * 8, 128), jnp.float32),
        scratch_shapes=[
            pltpu.VMEM((PAIR_ORB, STEP_SRC * SLOTS), jnp.bfloat16),
            pltpu.VMEM((PAIR_ORB, STEP_SRC * SLOTS), jnp.bfloat16),
            pltpu.VMEM((PAIR_ORB, PAIR_ORB), jnp.float32),
            pltpu.SMEM((ORBITS,), jnp.int32),
        ],
        compiler_params=pltpu.CompilerParams(vmem_limit_bytes=12 << 20),
        name="sum_pairs",
    )(hbm(crossing), pltpu.with_memory_space_constraint(arrived, pltpu.VMEM))


def place(arrived, crossing):
    return pl.pallas_call(
        place_kernel,
        in_specs=[smem(), in_vmem()],
        out_specs=in_vmem(),
        out_shape=jax.ShapeDtypeStruct((DEVICES * 8, 128), jnp.float32),
        scratch_shapes=[pltpu.VMEM((128, 128), jnp.float32)],
        compiler_params=pltpu.CompilerParams(vmem_limit_bytes=8 << 20),
        name="place",
    )(hbm(crossing), pltpu.with_memory_space_constraint(arrived, pltpu.VMEM))


def local(jacobians, point_normals, block_counts, pair_owner, pair_local, crossing):
    sent = make_blocks(
        jacobians, point_normals, block_counts.reshape(SLOTS), pair_owner.reshape(SLOTS), pair_local, crossing
    )
    arrived = exchange(sent.reshape(DEVICES, ROWS, 1, SLOTS))
    sums = sum_pairs(arrived.reshape(DEVICES * ROWS, SLOTS), crossing)
    mine = exchange(sums.reshape(DEVICES, 8, 128))
    out = place(mine.reshape(DEVICES * 8, 128), crossing)
    out = jnp.transpose(out.reshape(4, 32, 8, 128), (0, 2, 1, 3))
    return out.reshape(1, PAIR_ORB // TILES, PARAMS * PARAMS)


def solution(mesh):
    both = ("tile", "orbit")
    in_specs = (
        P(both, None, None, None),
        P(both, None, None),
        P(both, None),
        P(both, None),
        P(both),
        P(),
    )
    return jax.shard_map(local, mesh=mesh, in_specs=in_specs, out_specs=P("orbit", "tile", None), check_vma=False)
```

time: 107 us -> 80.8 us (0.76)
  Pallas kernels: 44.7 us -> 20.5 us
  blocking collectives: 61.5 us -> 60.1 us
    pallas_call x3, Pallas kernels: 44.7 us -> 20.5 us  [the longest x1 10.9 us: make_blocks(): pl.pallas_call(blocks_kernel, in_specs=[smem(), smem(), smem(), in_hbm(),...]
    all_to_all x2, blocking collectives: 61.5 us -> 60.1 us  [exchange(): lax.all_to_all(x, ('tile', 'orbit'), split_axis=0, concat_axis=0, tiled=T...]
where the time goes in v2:
time: 80.8 us; the launch traced here: 80.7 us
  blocking collectives  60.1 us (74%)
  Pallas kernels  20.5 us (25%)
    all_to_all x2, blocking collectives, exchange(): lax.all_to_all(x, ('tile', 'orbit'), split_axis=0, concat_axis=0, tiled=T...  60.1 us
    pallas_call x1, Pallas kernels, make_blocks(): pl.pallas_call(blocks_kernel, in_specs=[smem(), smem(), smem(), in_hbm(),...  10.9 us
    pallas_call x1, Pallas kernels, sum_pairs(): pl.pallas_call(sum_kernel, in_specs=[smem(), in_vmem()], out_specs=in_vme...  8 us
    pallas_call x1, Pallas kernels, place(): pl.pallas_call(place_kernel, in_specs=[smem(), in_vmem()], out_specs=in_v...  1.64 us

profile of v2, /device:TPU:1, one launch (start us, length us, event | category | flops | bytes accessed | tf_op | source)
XLA Modules:
  0.0 80.7 jit_solution(9497683361907415717)
XLA Ops:
  0.0 10.9 %blocks.1 = f32[4224,128]{1,0:T(8,128)S(1)} custom-call(s32[128]{0:T(128)} %bitcast.25, s32[128]{0:T(128)} %bitcast.23, s32[16]{0:T(128)} %cross.5, bf16[128,384,128]{2,1,0:T(8,128)(2,1)} %bitcast.21, f32[6,128,128]{2,1,0:T(8,128)} %bitcast.22, s32[1,128]{1,0:T(1,128)} %bitcast.24, s32[1,128]{1,0:T(1,128)} %bitcast.26), custom_call_target="tpu_custom_call" | custom-call | tf_op jit(solution)/shard_map/blocks/pallas_call | solution.py:207
  10.9 41.7 %all_to_all.10 = f32[128,33,1,128]{3,2,1,0:T(1,128)S(1)} all-to-all(f32[128,33,1,128]{3,2,1,0:T(1,128)S(1)} %bitcast.17), channel_id=1, replica_groups=mesh['tile'=8,'orbit'=16] {'tile','orbit'}, dimensions={0} | all-to-all | bytes 4325376 | tf_op jit(solution)/shard_map/all_to_all | solution.py:189
  52.6 8.0 %sum_pairs.1 = f32[1024,128]{1,0:T(8,128)S(1)} custom-call(s32[16]{0:T(128)} %cross.5, f32[4224,128]{1,0:T(8,128)S(1)} %bitcast.18), custom_call_target="tpu_custom_call" | custom-call | tf_op jit(solution)/shard_map/sum_pairs/pallas_call | solution.py:225
  60.6 18.5 %all_to_all.11 = f32[128,8,128]{2,1,0:T(8,128)S(1)} all-to-all(f32[128,8,128]{2,1,0:T(8,128)S(1)} %bitcast.20), channel_id=1, replica_groups=mesh['tile'=8,'orbit'=16] {'tile','orbit'}, dimensions={0} | all-to-all | bytes 1048576 | tf_op jit(solution)/shard_map/all_to_all | solution.py:189
  79.0 1.6 %place.1 = f32[1024,128]{1,0:T(8,128)} custom-call(s32[16]{0:T(128)} %cross.5, f32[1024,128]{1,0:T(8,128)S(1)} %bitcast.19), custom_call_target="tpu_custom_call" | custom-call | tf_op jit(solution)/shard_map/place/pallas_call | solution.py:242

commit v3 on v2

--- a/solution.py
+++ b/solution.py
@@ -15,7 +15,7 @@
 ELEMS = PARAMS * PARAMS // DEVICES
 ROWS = ELEMS + 1
 STEP_SLOTS = 8
-STEP_SRC = 16
+STEP_SRC = 64
 NT = (((1,), (1,)), ((), ()))
 
 
@@ -40,7 +40,7 @@
     return ranks[jnp.minimum(o, cross[o])]
 
 
-def blocks_kernel(counts, owner, cross, jac_hbm, normals_hbm, owner_row, local_row, out, jac, normals, held, ranks, sems):
+def blocks_kernel(counts, owner, cross, jac_hbm, normals_hbm, owner_row, local_row, out, jac, normals, held, planes, turned_a, turned_b, solved_a, solved_b, ranks, sems):
     steps = SLOTS // STEP_SLOTS
     copy_normals = pltpu.make_async_copy(normals_hbm, normals, sems.at[steps])
     copy_normals.start()
@@ -62,7 +62,13 @@
     sub = lax.broadcasted_iota(jnp.int32, (STEP_SLOTS, PTS), 0)
     place = lax.broadcasted_iota(jnp.int32, (STEP_SLOTS, PTS), 1)
 
-    def body(step, carry):
+    def turn(step, target):
+        base = pl.multiple_of(step * STEP_SLOTS, STEP_SLOTS)
+        for i in range(STEP_SLOTS):
+            for q in range(3):
+                target[i, q] = jac[base + i, q * PTS : (q + 1) * PTS, :].T
+
+    def solve(step, source, target):
         base = pl.multiple_of(step * STEP_SLOTS, STEP_SLOTS)
         w11, w22, w33, w12, w13, w23 = (normals[q, pl.ds(base, STEP_SLOTS), :] for q in range(6))
         c11 = w22 * w33 - w23 * w23
@@ -78,54 +84,68 @@
         weight = jnp.where(place < limit, 1.0, 0.0) / det
         c11, c22, c33 = c11 * weight, c22 * weight, c33 * weight
         c12, c13, c23 = c12 * weight, c13 * weight, c23 * weight
-        part(step).wait()
         for i in range(STEP_SLOTS):
-            slot = base + i
-            turned = jac[slot].T
-            left = turned[:PARAMS]
-            right = turned[PARAMS:].astype(jnp.float32)
-            one, two, three = right[:, :PTS], right[:, PTS : 2 * PTS], right[:, 2 * PTS :]
             row = slice(i, i + 1)
-            solved = jnp.concatenate(
-                [
-                    c11[row] * one + c12[row] * two + c13[row] * three,
-                    c12[row] * one + c22[row] * two + c23[row] * three,
-                    c13[row] * one + c23[row] * two + c33[row] * three,
-                ],
-                axis=1,
-            ).astype(jnp.bfloat16)
-            mine = owner[slot]
-            upper = mine > cross[mine]
-            a = jnp.where(upper, left, solved)
-            b = jnp.where(upper, solved, left)
-            held[pl.ds(slot, PARAMS, stride=SLOTS + 1), :] = dot_nt(a, b)
+            for first in range(0, PARAMS, 16):
+                at = slice(first, first + 16)
+                one, two, three = (source[i, q, PARAMS + first : PARAMS + first + 16, :].astype(jnp.float32) for q in range(3))
+                target[i, 0, at, :] = (c11[row] * one + c12[row] * two + c13[row] * three).astype(jnp.bfloat16)
+                target[i, 1, at, :] = (c12[row] * one + c22[row] * two + c23[row] * three).astype(jnp.bfloat16)
+                target[i, 2, at, :] = (c13[row] * one + c23[row] * two + c33[row] * three).astype(jnp.bfloat16)
+            block = dot_nt(jnp.concatenate([target[i, q] for q in range(3)], axis=1), jnp.concatenate([source[i, q, :PARAMS, :] for q in range(3)], axis=1))
+            held[pl.ds(base + i, PARAMS, stride=SLOTS + 1), :] = block
+
+    def body(pair, carry):
+        step = pair * 2
+        part(step + 1).wait()
+        turn(step + 1, turned_b)
+        solve(step, turned_a, solved_a)
+
+        @pl.when(step + 2 < steps)
+        def _():
+            part(step + 2).wait()
+
+        turn(jnp.minimum(step + 2, steps - 1), turned_a)
+        solve(step + 1, turned_b, solved_b)
         return carry
 
-    lax.fori_loop(0, steps, body, 0)
+    part(0).wait()
+    turn(0, turned_a)
+    lax.fori_loop(0, steps // 2, body, 0)
+    for line in range(PARAMS):
+        lines = held[line * (SLOTS + 1) : line * (SLOTS + 1) + SLOTS, :PARAMS].astype(jnp.bfloat16)
+        planes[pl.ds(line, PARAMS, stride=PARAMS + 1), :] = lines.T.astype(jnp.float32)
+    upper = jnp.zeros_like(names)
+    for o in range(ORBITS):
+        upper = jnp.where(names == o, (o > cross[o]).astype(jnp.int32), upper)
+    upper = jnp.broadcast_to(upper, (PARAMS, SLOTS)) == 1
     half = PARAMS // 2
     for col in range(PARAMS):
-        lines = held[col * (SLOTS + 1) : col * (SLOTS + 1) + SLOTS, :]
+        straight = planes[pl.ds(col, PARAMS, stride=PARAMS + 1), :]
+        flipped = planes[col * (PARAMS + 1) : col * (PARAMS + 1) + PARAMS, :]
         start = (col // half) * PARAMS * ROWS + col % half
-        out[pl.ds(start, PARAMS, stride=ROWS), :] = lines.T
+        out[pl.ds(start, PARAMS, stride=ROWS), :] = jnp.where(upper, flipped, straight)
 
 
 def sum_kernel(cross, arrived, out, hot, values, total, ranks):
-    lines = lax.broadcasted_iota(jnp.int32, (PAIR_ORB, SLOTS), 0)
+    lines = lax.broadcasted_iota(jnp.int32, (PAIR_ORB, SLOTS), 0).astype(jnp.bfloat16)
+    one = jnp.ones((PAIR_ORB, SLOTS), jnp.bfloat16)
+    none = jnp.zeros((PAIR_ORB, SLOTS), jnp.bfloat16)
     total[...] = jnp.zeros_like(total)
 
     def body(step, carry):
-        for i in range(STEP_SRC):
-            base = (step * STEP_SRC + i) * ROWS
-            piece = arrived[pl.ds(base, ELEMS), :]
-            ids = arrived[pl.ds(base + ELEMS, 1), :].astype(jnp.int32)
-            local = ids & (PAIR_ORB - 1)
-            line = (ids >> 8) * 32 + (local >> 6) * 8 + (local & 7)
-            group = (local >> 3) & 7
-            at = slice(i * SLOTS, (i + 1) * SLOTS)
-            hot[:, at] = jnp.where(lines == line, 1.0, 0.0).astype(jnp.bfloat16)
-            for g in range(8):
-                values[g * ELEMS : (g + 1) * ELEMS, at] = jnp.where(group == g, piece, 0.0).astype(jnp.bfloat16)
-        total[...] += dot_nt(hot[...], values[...])
+        for part in range(STEP_SRC // 64):
+            hots, vals = [], []
+            for i in range(64):
+                base = (step * STEP_SRC + part * 64 + i) * ROWS
+                piece = arrived[pl.ds(base, ELEMS), :].astype(jnp.bfloat16)
+                ids = arrived[pl.ds(base + ELEMS, 1), :].astype(jnp.int32)
+                local = ids & (PAIR_ORB - 1)
+                line = ((ids >> 8) * 32 + (local >> 6) * 8 + (local & 7)).astype(jnp.bfloat16)
+                group = jnp.broadcast_to(((local >> 3) & 7).astype(jnp.bfloat16), (ELEMS, SLOTS))
+                hots.append(jnp.where(lines == line, one, none))
+                vals.append(jnp.concatenate([jnp.where(group == g, piece, none[:ELEMS]) for g in range(8)], axis=0))
+            total[...] += dot_nt(jnp.concatenate(hots, axis=1), jnp.concatenate(vals, axis=1))
         return carry
 
     lax.fori_loop(0, DEVICES // STEP_SRC, body, 0)
@@ -213,6 +233,11 @@
             pltpu.VMEM((SLOTS, 3 * PTS, 2 * PARAMS), jnp.bfloat16),
             pltpu.VMEM((6, SLOTS, PTS), jnp.float32),
             pltpu.VMEM((PARAMS * (SLOTS + 1), PARAMS), jnp.float32),
+            pltpu.VMEM((PARAMS * (PARAMS + 1), SLOTS), jnp.float32),
+            pltpu.VMEM((STEP_SLOTS, 3, 2 * PARAMS, PTS), jnp.bfloat16),
+            pltpu.VMEM((STEP_SLOTS, 3, 2 * PARAMS, PTS), jnp.bfloat16),
+            pltpu.VMEM((STEP_SLOTS, 3, PARAMS, PTS), jnp.bfloat16),
+            pltpu.VMEM((STEP_SLOTS, 3, PARAMS, PTS), jnp.bfloat16),
             pltpu.SMEM((ORBITS,), jnp.int32),
             pltpu.SemaphoreType.DMA((SLOTS // STEP_SLOTS + 1,)),
         ],
@@ -233,7 +258,7 @@
             pltpu.VMEM((PAIR_ORB, PAIR_ORB), jnp.float32),
             pltpu.SMEM((ORBITS,), jnp.int32),
         ],
-        compiler_params=pltpu.CompilerParams(vmem_limit_bytes=12 << 20),
+        compiler_params=pltpu.CompilerParams(vmem_limit_bytes=24 << 20),
         name="sum_pairs",
     )(hbm(crossing), pltpu.with_memory_space_constraint(arrived, pltpu.VMEM))
 

time: 80.8 us -> 75.4 us (0.933)
  Pallas kernels: 20.5 us -> 15.1 us
    pallas_call x1, Pallas kernels: 8 us -> 3.38 us  [sum_pairs(): pl.pallas_call(sum_kernel, in_specs=[smem(), in_vmem()], out_specs=in_vme...]
    pallas_call x1, Pallas kernels: 10.9 us -> 10 us  [make_blocks(): pl.pallas_call(blocks_kernel, in_specs=[smem(), smem(), smem(), in_hbm(),...]
where the time goes in v3:
time: 75.4 us; the launch traced here: 75.2 us
  blocking collectives  60.1 us (80%)
  Pallas kernels  15.1 us (20%)
    all_to_all x2, blocking collectives, exchange(): lax.all_to_all(x, ('tile', 'orbit'), split_axis=0, concat_axis=0, tiled=T...  60.1 us
    pallas_call x1, Pallas kernels, make_blocks(): pl.pallas_call(blocks_kernel, in_specs=[smem(), smem(), smem(), in_hbm(),...  10 us
    pallas_call x1, Pallas kernels, sum_pairs(): pl.pallas_call(sum_kernel, in_specs=[smem(), in_vmem()], out_specs=in_vme...  3.38 us
    pallas_call x1, Pallas kernels, place(): pl.pallas_call(place_kernel, in_specs=[smem(), in_vmem()], out_specs=in_v...  1.64 us

profile of v3, /device:TPU:1, one launch (start us, length us, event | category | flops | bytes accessed | tf_op | source)
XLA Modules:
  0.0 75.2 jit_solution(12604523580117675881)
XLA Ops:
  0.0 10.0 %blocks.1 = f32[4224,128]{1,0:T(8,128)S(1)} custom-call(s32[128]{0:T(128)} %bitcast.25, s32[128]{0:T(128)} %bitcast.23, s32[16]{0:T(128)} %cross.5, bf16[128,384,128]{2,1,0:T(8,128)(2,1)} %bitcast.21, f32[6,128,128]{2,1,0:T(8,128)} %bitcast.22, s32[1,128]{1,0:T(1,128)} %bitcast.24, s32[1,128]{1,0:T(1,128)} %bitcast.26), custom_call_target="tpu_custom_call" | custom-call | tf_op jit(solution)/shard_map/blocks/pallas_call | solution.py:227
  10.1 41.7 %all_to_all.10 = f32[128,33,1,128]{3,2,1,0:T(1,128)S(1)} all-to-all(f32[128,33,1,128]{3,2,1,0:T(1,128)S(1)} %bitcast.17), channel_id=1, replica_groups=mesh['tile'=8,'orbit'=16] {'tile','orbit'}, dimensions={0} | all-to-all | bytes 4325376 | tf_op jit(solution)/shard_map/all_to_all | solution.py:209
  51.7 3.4 %sum_pairs.1 = f32[1024,128]{1,0:T(8,128)S(1)} custom-call(s32[16]{0:T(128)} %cross.5, f32[4224,128]{1,0:T(8,128)S(1)} %bitcast.18), custom_call_target="tpu_custom_call" | custom-call | tf_op jit(solution)/shard_map/sum_pairs/pallas_call | solution.py:250
  55.1 18.5 %all_to_all.11 = f32[128,8,128]{2,1,0:T(8,128)S(1)} all-to-all(f32[128,8,128]{2,1,0:T(8,128)S(1)} %bitcast.20), channel_id=1, replica_groups=mesh['tile'=8,'orbit'=16] {'tile','orbit'}, dimensions={0} | all-to-all | bytes 1048576 | tf_op jit(solution)/shard_map/all_to_all | solution.py:209
  73.6 1.6 %place.1 = f32[1024,128]{1,0:T(8,128)} custom-call(s32[16]{0:T(128)} %cross.5, f32[1024,128]{1,0:T(8,128)S(1)} %bitcast.19), custom_call_target="tpu_custom_call" | custom-call | tf_op jit(solution)/shard_map/place/pallas_call | solution.py:267

commit v4 on v3

--- a/solution.py
+++ b/solution.py
@@ -15,7 +15,7 @@
 ELEMS = PARAMS * PARAMS // DEVICES
 ROWS = ELEMS + 1
 STEP_SLOTS = 8
-STEP_SRC = 64
+STEP_SRC = 128
 NT = (((1,), (1,)), ((), ()))
 
 
@@ -40,16 +40,16 @@
     return ranks[jnp.minimum(o, cross[o])]
 
 
-def blocks_kernel(counts, owner, cross, jac_hbm, normals_hbm, owner_row, local_row, out, jac, normals, held, planes, turned_a, turned_b, solved_a, solved_b, ranks, sems):
+def blocks_kernel(counts, owner, cross, jac_hbm, normals_hbm, owner_row, local_row, out, jac, normals, held, planes, turned_a, turned_b, left_a, left_b, solved_a, solved_b, ranks, sems):
     steps = SLOTS // STEP_SLOTS
     copy_normals = pltpu.make_async_copy(normals_hbm, normals, sems.at[steps])
     copy_normals.start()
 
     def part(step):
-        at = pl.ds(step * STEP_SLOTS, STEP_SLOTS)
+        at = pl.ds(step * (2 * STEP_SLOTS), 2 * STEP_SLOTS)
         return pltpu.make_async_copy(jac_hbm.at[at], jac.at[at], sems.at[step])
 
-    for step in range(steps):
+    for step in range(steps // 2):
         part(step).start()
     crossing_ranks(cross, ranks)
     names = owner_row[...]
@@ -62,13 +62,15 @@
     sub = lax.broadcasted_iota(jnp.int32, (STEP_SLOTS, PTS), 0)
     place = lax.broadcasted_iota(jnp.int32, (STEP_SLOTS, PTS), 1)
 
-    def turn(step, target):
+    def turn(step, target, left):
         base = pl.multiple_of(step * STEP_SLOTS, STEP_SLOTS)
         for i in range(STEP_SLOTS):
             for q in range(3):
-                target[i, q] = jac[base + i, q * PTS : (q + 1) * PTS, :].T
-
-    def solve(step, source, target):
+                both = jac[base + i, q * PTS : (q + 1) * PTS, :].T
+                target[i, q] = both[PARAMS:].astype(jnp.float32)
+                left[i, q] = both[:PARAMS]
+
+    def solve(step, source, left, target):
         base = pl.multiple_of(step * STEP_SLOTS, STEP_SLOTS)
         w11, w22, w33, w12, w13, w23 = (normals[q, pl.ds(base, STEP_SLOTS), :] for q in range(6))
         c11 = w22 * w33 - w23 * w23
@@ -88,30 +90,26 @@
             row = slice(i, i + 1)
             for first in range(0, PARAMS, 16):
                 at = slice(first, first + 16)
-                one, two, three = (source[i, q, PARAMS + first : PARAMS + first + 16, :].astype(jnp.float32) for q in range(3))
+                one, two, three = (source[i, q, at, :] for q in range(3))
                 target[i, 0, at, :] = (c11[row] * one + c12[row] * two + c13[row] * three).astype(jnp.bfloat16)
                 target[i, 1, at, :] = (c12[row] * one + c22[row] * two + c23[row] * three).astype(jnp.bfloat16)
                 target[i, 2, at, :] = (c13[row] * one + c23[row] * two + c33[row] * three).astype(jnp.bfloat16)
-            block = dot_nt(jnp.concatenate([target[i, q] for q in range(3)], axis=1), jnp.concatenate([source[i, q, :PARAMS, :] for q in range(3)], axis=1))
+            block = dot_nt(jnp.concatenate([target[i, q] for q in range(3)], axis=1), jnp.concatenate([left[i, q] for q in range(3)], axis=1))
             held[pl.ds(base + i, PARAMS, stride=SLOTS + 1), :] = block
 
     def body(pair, carry):
         step = pair * 2
-        part(step + 1).wait()
-        turn(step + 1, turned_b)
-        solve(step, turned_a, solved_a)
-
-        @pl.when(step + 2 < steps)
-        def _():
-            part(step + 2).wait()
-
-        turn(jnp.minimum(step + 2, steps - 1), turned_a)
-        solve(step + 1, turned_b, solved_b)
+        part(pair).wait()
+        turn(step, turned_a, left_a)
+        solve(jnp.maximum(step - 1, 0), turned_b, left_b, solved_b)
+        turn(step + 1, turned_b, left_b)
+        solve(step, turned_a, left_a, solved_a)
         return carry
 
-    part(0).wait()
-    turn(0, turned_a)
+    turned_b[...] = jnp.zeros_like(turned_b)
+    left_b[...] = jnp.zeros_like(left_b)
     lax.fori_loop(0, steps // 2, body, 0)
+    solve(steps - 1, turned_b, left_b, solved_b)
     for line in range(PARAMS):
         lines = held[line * (SLOTS + 1) : line * (SLOTS + 1) + SLOTS, :PARAMS].astype(jnp.bfloat16)
         planes[pl.ds(line, PARAMS, stride=PARAMS + 1), :] = lines.T.astype(jnp.float32)
@@ -134,10 +132,10 @@
     total[...] = jnp.zeros_like(total)
 
     def body(step, carry):
-        for part in range(STEP_SRC // 64):
+        for part in range(STEP_SRC // 128):
             hots, vals = [], []
-            for i in range(64):
-                base = (step * STEP_SRC + part * 64 + i) * ROWS
+            for i in range(128):
+                base = (step * STEP_SRC + part * 128 + i) * ROWS
                 piece = arrived[pl.ds(base, ELEMS), :].astype(jnp.bfloat16)
                 ids = arrived[pl.ds(base + ELEMS, 1), :].astype(jnp.int32)
                 local = ids & (PAIR_ORB - 1)
@@ -234,14 +232,16 @@
             pltpu.VMEM((6, SLOTS, PTS), jnp.float32),
             pltpu.VMEM((PARAMS * (SLOTS + 1), PARAMS), jnp.float32),
             pltpu.VMEM((PARAMS * (PARAMS + 1), SLOTS), jnp.float32),
-            pltpu.VMEM((STEP_SLOTS, 3, 2 * PARAMS, PTS), jnp.bfloat16),
-            pltpu.VMEM((STEP_SLOTS, 3, 2 * PARAMS, PTS), jnp.bfloat16),
+            pltpu.VMEM((STEP_SLOTS, 3, PARAMS, PTS), jnp.float32),
+            pltpu.VMEM((STEP_SLOTS, 3, PARAMS, PTS), jnp.float32),
+            pltpu.VMEM((STEP_SLOTS, 3, PARAMS, PTS), jnp.bfloat16),
+            pltpu.VMEM((STEP_SLOTS, 3, PARAMS, PTS), jnp.bfloat16),
             pltpu.VMEM((STEP_SLOTS, 3, PARAMS, PTS), jnp.bfloat16),
             pltpu.VMEM((STEP_SLOTS, 3, PARAMS, PTS), jnp.bfloat16),
             pltpu.SMEM((ORBITS,), jnp.int32),
             pltpu.SemaphoreType.DMA((SLOTS // STEP_SLOTS + 1,)),
         ],
-        compiler_params=pltpu.CompilerParams(vmem_limit_bytes=24 << 20),
+        compiler_params=pltpu.CompilerParams(vmem_limit_bytes=28 << 20),
         name="blocks",
     )(*map(hbm, (counts, owners, crossing, jac, normals, owners.reshape(1, SLOTS), locals_.reshape(1, SLOTS))))
 
@@ -258,7 +258,7 @@
             pltpu.VMEM((PAIR_ORB, PAIR_ORB), jnp.float32),
             pltpu.SMEM((ORBITS,), jnp.int32),
         ],
-        compiler_params=pltpu.CompilerParams(vmem_limit_bytes=24 << 20),
+        compiler_params=pltpu.CompilerParams(vmem_limit_bytes=28 << 20),
         name="sum_pairs",
     )(hbm(crossing), pltpu.with_memory_space_constraint(arrived, pltpu.VMEM))
 

time: 75.4 us -> 74.2 us (0.984)
  Pallas kernels: 15.1 us -> 13.9 us
    pallas_call x1, Pallas kernels: 10 us -> 9.17 us  [make_blocks(): pl.pallas_call(blocks_kernel, in_specs=[smem(), smem(), smem(), in_hbm(),...]
where the time goes in v4:
time: 74.2 us; the launch traced here: 74 us
  blocking collectives  60.1 us (81%)
  Pallas kernels  13.9 us (19%)
    all_to_all x2, blocking collectives, exchange(): lax.all_to_all(x, ('tile', 'orbit'), split_axis=0, concat_axis=0, tiled=T...  60.1 us
    pallas_call x1, Pallas kernels, make_blocks(): pl.pallas_call(blocks_kernel, in_specs=[smem(), smem(), smem(), in_hbm(),...  9.17 us
    pallas_call x1, Pallas kernels, sum_pairs(): pl.pallas_call(sum_kernel, in_specs=[smem(), in_vmem()], out_specs=in_vme...  3.08 us
    pallas_call x1, Pallas kernels, place(): pl.pallas_call(place_kernel, in_specs=[smem(), in_vmem()], out_specs=in_v...  1.64 us

profile of v4, /device:TPU:1, one launch (start us, length us, event | category | flops | bytes accessed | tf_op | source)
XLA Modules:
  0.0 74.0 jit_solution(15494365646365531220)
XLA Ops:
  0.0 9.2 %blocks.1 = f32[4224,128]{1,0:T(8,128)S(1)} custom-call(s32[128]{0:T(128)} %bitcast.25, s32[128]{0:T(128)} %bitcast.23, s32[16]{0:T(128)} %cross.5, bf16[128,384,128]{2,1,0:T(8,128)(2,1)} %bitcast.21, f32[6,128,128]{2,1,0:T(8,128)} %bitcast.22, s32[1,128]{1,0:T(1,128)} %bitcast.24, s32[1,128]{1,0:T(1,128)} %bitcast.26), custom_call_target="tpu_custom_call" | custom-call | tf_op jit(solution)/shard_map/blocks/pallas_call | solution.py:225
  9.2 41.7 %all_to_all.10 = f32[128,33,1,128]{3,2,1,0:T(1,128)S(1)} all-to-all(f32[128,33,1,128]{3,2,1,0:T(1,128)S(1)} %bitcast.17), channel_id=1, replica_groups=mesh['tile'=8,'orbit'=16] {'tile','orbit'}, dimensions={0} | all-to-all | bytes 4325376 | tf_op jit(solution)/shard_map/all_to_all | solution.py:207
  50.9 3.1 %sum_pairs.1 = f32[1024,128]{1,0:T(8,128)S(1)} custom-call(s32[16]{0:T(128)} %cross.5, f32[4224,128]{1,0:T(8,128)S(1)} %bitcast.18), custom_call_target="tpu_custom_call" | custom-call | tf_op jit(solution)/shard_map/sum_pairs/pallas_call | solution.py:250
  53.9 18.5 %all_to_all.11 = f32[128,8,128]{2,1,0:T(8,128)S(1)} all-to-all(f32[128,8,128]{2,1,0:T(8,128)S(1)} %bitcast.20), channel_id=1, replica_groups=mesh['tile'=8,'orbit'=16] {'tile','orbit'}, dimensions={0} | all-to-all | bytes 1048576 | tf_op jit(solution)/shard_map/all_to_all | solution.py:207
  72.4 1.6 %place.1 = f32[1024,128]{1,0:T(8,128)} custom-call(s32[16]{0:T(128)} %cross.5, f32[1024,128]{1,0:T(8,128)S(1)} %bitcast.19), custom_call_target="tpu_custom_call" | custom-call | tf_op jit(solution)/shard_map/place/pallas_call | solution.py:267

commit v5 on v4

--- a/solution.py
+++ b/solution.py
@@ -59,16 +59,18 @@
     ids = (ids + local_row[...]).astype(jnp.float32)
     out[pl.ds(ELEMS, DEVICES, stride=ROWS), :] = jnp.broadcast_to(ids, (DEVICES, SLOTS))
     copy_normals.wait()
+    ident = eye(2 * PARAMS)
     sub = lax.broadcasted_iota(jnp.int32, (STEP_SLOTS, PTS), 0)
     place = lax.broadcasted_iota(jnp.int32, (STEP_SLOTS, PTS), 1)
 
-    def turn(step, target, left):
+    def turn(step, target, left, late):
         base = pl.multiple_of(step * STEP_SLOTS, STEP_SLOTS)
         for i in range(STEP_SLOTS):
             for q in range(3):
-                both = jac[base + i, q * PTS : (q + 1) * PTS, :].T
+                piece = jac[base + i, q * PTS : (q + 1) * PTS, :]
+                both = dot_nt(ident, piece) if late and i >= 6 else piece.T
                 target[i, q] = both[PARAMS:].astype(jnp.float32)
-                left[i, q] = both[:PARAMS]
+                left[i, q] = both[:PARAMS].astype(jnp.bfloat16)
 
     def solve(step, source, left, target):
         base = pl.multiple_of(step * STEP_SLOTS, STEP_SLOTS)
@@ -100,9 +102,9 @@
     def body(pair, carry):
         step = pair * 2
         part(pair).wait()
-        turn(step, turned_a, left_a)
+        turn(step, turned_a, left_a, False)
         solve(jnp.maximum(step - 1, 0), turned_b, left_b, solved_b)
-        turn(step + 1, turned_b, left_b)
+        turn(step + 1, turned_b, left_b, True)
         solve(step, turned_a, left_a, solved_a)
         return carry
 

time: 74.2 us -> 73.9 us (level)
  no operation moved by 1% of the time
where the time goes in v5:
time: 73.9 us; the launch traced here: 73.7 us
  blocking collectives  60.1 us (81%)
  Pallas kernels  13.5 us (18%)
    all_to_all x2, blocking collectives, exchange(): lax.all_to_all(x, ('tile', 'orbit'), split_axis=0, concat_axis=0, tiled=T...  60.1 us
    pallas_call x1, Pallas kernels, make_blocks(): pl.pallas_call(blocks_kernel, in_specs=[smem(), smem(), smem(), in_hbm(),...  8.81 us
    pallas_call x1, Pallas kernels, sum_pairs(): pl.pallas_call(sum_kernel, in_specs=[smem(), in_vmem()], out_specs=in_vme...  3.08 us
    pallas_call x1, Pallas kernels, place(): pl.pallas_call(place_kernel, in_specs=[smem(), in_vmem()], out_specs=in_v...  1.64 us

profile of v5, /device:TPU:1, one launch (start us, length us, event | category | flops | bytes accessed | tf_op | source)
XLA Modules:
  0.0 73.7 jit_solution(11688219616555201930)
XLA Ops:
  0.0 8.8 %blocks.1 = f32[4224,128]{1,0:T(8,128)S(1)} custom-call(s32[128]{0:T(128)} %bitcast.25, s32[128]{0:T(128)} %bitcast.23, s32[16]{0:T(128)} %cross.5, bf16[128,384,128]{2,1,0:T(8,128)(2,1)} %bitcast.21, f32[6,128,128]{2,1,0:T(8,128)} %bitcast.22, s32[1,128]{1,0:T(1,128)} %bitcast.24, s32[1,128]{1,0:T(1,128)} %bitcast.26), custom_call_target="tpu_custom_call" | custom-call | tf_op jit(solution)/shard_map/blocks/pallas_call | solution.py:227
  8.8 41.7 %all_to_all.10 = f32[128,33,1,128]{3,2,1,0:T(1,128)S(1)} all-to-all(f32[128,33,1,128]{3,2,1,0:T(1,128)S(1)} %bitcast.17), channel_id=1, replica_groups=mesh['tile'=8,'orbit'=16] {'tile','orbit'}, dimensions={0} | all-to-all | bytes 4325376 | tf_op jit(solution)/shard_map/all_to_all | solution.py:209
  50.5 3.1 %sum_pairs.1 = f32[1024,128]{1,0:T(8,128)S(1)} custom-call(s32[16]{0:T(128)} %cross.5, f32[4224,128]{1,0:T(8,128)S(1)} %bitcast.18), custom_call_target="tpu_custom_call" | custom-call | tf_op jit(solution)/shard_map/sum_pairs/pallas_call | solution.py:252
  53.6 18.5 %all_to_all.11 = f32[128,8,128]{2,1,0:T(8,128)S(1)} all-to-all(f32[128,8,128]{2,1,0:T(8,128)S(1)} %bitcast.20), channel_id=1, replica_groups=mesh['tile'=8,'orbit'=16] {'tile','orbit'}, dimensions={0} | all-to-all | bytes 1048576 | tf_op jit(solution)/shard_map/all_to_all | solution.py:209
  72.1 1.6 %place.1 = f32[1024,128]{1,0:T(8,128)} custom-call(s32[16]{0:T(128)} %cross.5, f32[1024,128]{1,0:T(8,128)S(1)} %bitcast.19), custom_call_target="tpu_custom_call" | custom-call | tf_op jit(solution)/shard_map/place/pallas_call | solution.py:269

commit v6 on v5

--- a/solution.py
+++ b/solution.py
@@ -68,7 +68,7 @@
         for i in range(STEP_SLOTS):
             for q in range(3):
                 piece = jac[base + i, q * PTS : (q + 1) * PTS, :]
-                both = dot_nt(ident, piece) if late and i >= 6 else piece.T
+                both = dot_nt(ident, piece) if late and (i >= 6 or (i == 5 and q == 2)) else piece.T
                 target[i, q] = both[PARAMS:].astype(jnp.float32)
                 left[i, q] = both[:PARAMS].astype(jnp.bfloat16)
 

time: 73.9 us -> 73.8 us (level)
  no operation moved by 1% of the time
where the time goes in v6:
time: 73.8 us; the launch traced here: 73.6 us
  blocking collectives  60.1 us (81%)
  Pallas kernels  13.4 us (18%)
    all_to_all x2, blocking collectives, exchange(): lax.all_to_all(x, ('tile', 'orbit'), split_axis=0, concat_axis=0, tiled=T...  60.1 us
    pallas_call x1, Pallas kernels, make_blocks(): pl.pallas_call(blocks_kernel, in_specs=[smem(), smem(), smem(), in_hbm(),...  8.71 us
    pallas_call x1, Pallas kernels, sum_pairs(): pl.pallas_call(sum_kernel, in_specs=[smem(), in_vmem()], out_specs=in_vme...  3.08 us
    pallas_call x1, Pallas kernels, place(): pl.pallas_call(place_kernel, in_specs=[smem(), in_vmem()], out_specs=in_v...  1.64 us

profile of v6, /device:TPU:1, one launch (start us, length us, event | category | flops | bytes accessed | tf_op | source)
XLA Modules:
  0.0 73.6 jit_solution(5808271601576583196)
XLA Ops:
  0.0 8.7 %blocks.1 = f32[4224,128]{1,0:T(8,128)S(1)} custom-call(s32[128]{0:T(128)} %bitcast.25, s32[128]{0:T(128)} %bitcast.23, s32[16]{0:T(128)} %cross.5, bf16[128,384,128]{2,1,0:T(8,128)(2,1)} %bitcast.21, f32[6,128,128]{2,1,0:T(8,128)} %bitcast.22, s32[1,128]{1,0:T(1,128)} %bitcast.24, s32[1,128]{1,0:T(1,128)} %bitcast.26), custom_call_target="tpu_custom_call" | custom-call | tf_op jit(solution)/shard_map/blocks/pallas_call | solution.py:227
  8.7 41.7 %all_to_all.10 = f32[128,33,1,128]{3,2,1,0:T(1,128)S(1)} all-to-all(f32[128,33,1,128]{3,2,1,0:T(1,128)S(1)} %bitcast.17), channel_id=1, replica_groups=mesh['tile'=8,'orbit'=16] {'tile','orbit'}, dimensions={0} | all-to-all | bytes 4325376 | tf_op jit(solution)/shard_map/all_to_all | solution.py:209
  50.4 3.1 %sum_pairs.1 = f32[1024,128]{1,0:T(8,128)S(1)} custom-call(s32[16]{0:T(128)} %cross.5, f32[4224,128]{1,0:T(8,128)S(1)} %bitcast.18), custom_call_target="tpu_custom_call" | custom-call | tf_op jit(solution)/shard_map/sum_pairs/pallas_call | solution.py:252
  53.5 18.5 %all_to_all.11 = f32[128,8,128]{2,1,0:T(8,128)S(1)} all-to-all(f32[128,8,128]{2,1,0:T(8,128)S(1)} %bitcast.20), channel_id=1, replica_groups=mesh['tile'=8,'orbit'=16] {'tile','orbit'}, dimensions={0} | all-to-all | bytes 1048576 | tf_op jit(solution)/shard_map/all_to_all | solution.py:209
  72.0 1.6 %place.1 = f32[1024,128]{1,0:T(8,128)} custom-call(s32[16]{0:T(128)} %cross.5, f32[1024,128]{1,0:T(8,128)S(1)} %bitcast.19), custom_call_target="tpu_custom_call" | custom-call | tf_op jit(solution)/shard_map/place/pallas_call | solution.py:269
